TPU v7x, 32 devices: a whole 2x2x4 slice. The times are simulated.
32 devices in a mesh: dp: 4 (over z), mp: 8 (over y, x, core).
Axes of the slice: x: 2, y: 2, z: 4, core: 2. Of those that a mesh axis runs over, the one named last changes fastest.
Arguments:
- features: bfloat16 [256, 256, 1, 16, 64], P('mp', None, None, 'dp'), may hold values from -6 to 6
- out_grad: bfloat16 [256, 256, 1, 16, 64], P('mp', None, None, 'dp'), may hold values from -6 to 6
- spectral_weight: bfloat16 [16, 32, 32, 64, 128], P('dp', 'mp'), may hold values from -1.5 to 1.5
- local_weight: bfloat16 [64, 64], replicated, may hold values from -0.75 to 0.75
Outputs:
- layer_out: bfloat16 [256, 256, 1, 16, 64], P('mp', None, None, 'dp')
- feature_grad: bfloat16 [256, 256, 1, 16, 64], P('mp', None, None, 'dp')
- spectral_grad: float32 [16, 32, 32, 64, 128], P('dp', 'mp')
- local_grad: float32 [64, 64], replicated
All inputs are finite; a program needn't handle non-finite values.
Results may differ from a plain program's by a relative error of at most 0.03.
Values may be sent and summed in bfloat16 or wider, within the bound.
No kernel may reach another device: no remote copies, remote signals or barrier semaphores. Data moves between devices by JAX's collectives and lax.ppermute only.
A program may use at most 192 MiB of HBM per device.

v0:
```python
import math
import jax
import jax.numpy as jnp
from jax import lax
from jax.sharding import PartitionSpec as P

NX = 256
NY = 256
KX = 32
KY = 32
SNAP = 1


def make_tables(slab_count):
    y_index = jnp.arange(NY, dtype=jnp.int32)
    k_index = jnp.arange(KY, dtype=jnp.int32)
    y_angle = 2.0 * math.pi / NY * (k_index[:, None] * y_index[None, :] % NY).astype(jnp.float32)
    y_scale = 1.0 / math.sqrt(NY)
    y_table = jnp.stack([jnp.cos(y_angle) * y_scale, -jnp.sin(y_angle) * y_scale]).astype(
        jnp.bfloat16
    )
    k_weight = jnp.where(k_index == 0, 1.0, 2.0).astype(jnp.float32)
    y_back = (jnp.transpose(y_table.astype(jnp.float32), (2, 0, 1)) * k_weight).astype(jnp.bfloat16)
    stored_index = jnp.arange(NX, dtype=jnp.int32)
    slab_rows = NX // slab_count
    x_index = stored_index % slab_rows * slab_count + stored_index // slab_rows
    frequency = jnp.arange(KX, dtype=jnp.int32) - KX // 2
    x_angle = 2.0 * math.pi / NX * (frequency[:, None] * x_index[None, :] % NX).astype(jnp.float32)
    x_scale = 1.0 / math.sqrt(NX)
    x_cosine = jnp.cos(x_angle) * x_scale
    x_sine = jnp.sin(x_angle) * x_scale
    x_table = jnp.stack(
        [jnp.stack([x_cosine, x_sine], 1), jnp.stack([-x_sine, x_cosine], 1)]
    ).astype(jnp.bfloat16)
    x_back = jnp.transpose(x_table, (2, 3, 0, 1))
    return (y_table, y_back, x_table, x_back)


def product(form, left, right):
    return jnp.einsum(form, left, right, preferred_element_type=jnp.float32)


def block_weights(weights):
    channels = weights.shape[-1] // 2
    w_real = weights[..., :channels]
    w_imag = weights[..., channels:]
    upper = jnp.concatenate([w_real, w_imag], -1)
    lower = jnp.concatenate([-w_imag, w_real], -1)
    return jnp.concatenate([upper, lower], -2)


def to_items(coeffs, snaps, zcount):
    mode_rows, _, kx_count, columns = coeffs.shape
    channels = columns // (snaps * zcount)
    shaped = coeffs.reshape(mode_rows, 2, kx_count, snaps, zcount, channels).transpose(
        4, 0, 2, 3, 1, 5
    )
    return shaped.reshape(zcount, mode_rows * kx_count, snaps, 2 * channels)


def from_items(mode_items, mode_rows, snaps):
    zcount, total, _, double = mode_items.shape
    channels = double // 2
    kx_count = total // mode_rows
    shaped = mode_items.reshape(zcount, mode_rows, kx_count, snaps, 2, channels).transpose(
        1, 4, 2, 3, 0, 5
    )
    return shaped.reshape(mode_rows, 2, kx_count, snaps * zcount * channels)


def combine(gram_blocks, mode_rows):
    channels = gram_blocks.shape[-1] // 2
    top_left = gram_blocks[..., :channels, :channels]
    top_right = gram_blocks[..., :channels, channels:]
    low_left = gram_blocks[..., channels:, :channels]
    low_right = gram_blocks[..., channels:, channels:]
    joined = jnp.concatenate([top_left + low_right, top_right - low_left], -1)
    return joined.reshape(gram_blocks.shape[0], mode_rows, -1, channels, 2 * channels)


def activation(values):
    return jax.nn.gelu(values, approximate=True)


def body(features, out_grad, spectral_weight, local_weight):
    y_table, y_back, x_table, x_back = make_tables(lax.axis_size("mp"))
    rows_here, grid_y, snaps, zcount, channels = features.shape
    columns = snaps * zcount * channels
    mode_rows = spectral_weight.shape[1]
    offset = lax.axis_index("mp") * rows_here
    x_back_own = lax.dynamic_slice_in_dim(x_back, offset, rows_here, 1)
    x_table_own = lax.dynamic_slice_in_dim(x_table, offset, rows_here, 3)

    def to_modes(spectrum):
        return lax.psum_scatter(
            product("ojrx,xrkq->kojq", x_table_own, spectrum).astype(jnp.bfloat16),
            "mp",
            scatter_dimension=0,
            tiled=True,
        )

    def to_rows(coeffs):
        return product(
            "rxoj,kojq->xrkq", x_back_own, lax.all_gather(coeffs, "mp", axis=0, tiled=True)
        ).astype(jnp.bfloat16)

    flat_field = features.reshape(rows_here, grid_y, columns)
    spectrum_y = product("xyq,rky->xrkq", flat_field, y_table).astype(jnp.bfloat16)
    mode_coeffs = to_modes(spectrum_y)
    blocks = block_weights(spectral_weight).reshape(zcount, -1, 2 * channels, 2 * channels)
    mode_items = to_items(mode_coeffs, snaps, zcount)
    mixed_items = product("zmpi,zmio->zmpo", mode_items, blocks).astype(jnp.bfloat16)
    grid_rows = to_rows(from_items(mixed_items, mode_rows, snaps))
    local_part = jnp.dot(
        features.reshape(-1, channels), local_weight, preferred_element_type=jnp.float32
    )
    preact = product("yrk,xrkq->xyq", y_back, grid_rows) + local_part.reshape(
        rows_here, grid_y, columns
    )
    output, pullback = jax.vjp(activation, preact)
    preact_grad = pullback(out_grad.reshape(rows_here, grid_y, columns).astype(jnp.float32))[
        0
    ].astype(jnp.bfloat16)
    local_term = jnp.dot(
        features.reshape(-1, channels).T,
        preact_grad.reshape(-1, channels),
        preferred_element_type=jnp.float32,
    )
    grad_scale = 1.0 / math.sqrt(NX * NY * SNAP * lax.axis_size("dp") * zcount)
    local_grad = lax.psum(local_term, ("dp", "mp")) * grad_scale
    rows_grad = product("yrk,xyq->xrkq", y_back, preact_grad).astype(jnp.bfloat16)
    mixed_grad = to_modes(rows_grad)
    grad_items = to_items(mixed_grad, snaps, zcount)
    gram_blocks = product("zmpi,zmpo->zmio", mode_items, grad_items)
    spectral_grad = combine(gram_blocks, mode_rows)
    back_items = product("zmpo,zmio->zmpi", grad_items, blocks).astype(jnp.bfloat16)
    spectrum_grad = to_rows(from_items(back_items, mode_rows, snaps))
    local_back = jnp.dot(
        preact_grad.reshape(-1, channels), local_weight.T, preferred_element_type=jnp.float32
    )
    back_field = product("rky,xrkq->xyq", y_table, spectrum_grad) + local_back.reshape(
        rows_here, grid_y, columns
    )
    layer_out = output.astype(jnp.bfloat16).reshape(features.shape)
    feature_grad = back_field.astype(jnp.bfloat16).reshape(features.shape)
    return (layer_out, feature_grad, spectral_grad, local_grad)


def solution(mesh):
    placed = (
        P("mp", None, None, "dp", None),
        P("mp", None, None, "dp", None),
        P("dp", "mp", None, None, None),
        P(),
    )
    return jax.shard_map(
        body,
        mesh=mesh,
        in_specs=placed,
        out_specs=(
            P("mp", None, None, "dp", None),
            P("mp", None, None, "dp", None),
            P("dp", "mp", None, None, None),
            P(),
        ),
        check_vma=False,
    )
```

profile of v0, /device:TPU:0, one launch (start us, length us, event | category | flops | bytes accessed | tf_op | source)
XLA Modules:
  0.0 325.2 jit_solution(8694081158683600945)
XLA Ops:
  7.7 3.6 %fusion.16 = bf16[32,2,32,256,1]{3,2,0,1,4:T(8,128)(2,1)S(1)} fusion(bf16[32,256,256,1]{1,2,0,3:T(8,128)(2,1)} %bitcast.172, bf16[1,32,256]{2,1,0:T(8,128)(2,1)S(1)} %get-tuple-element.31, bf16[1,32,256]{2,1,0:T(8,128)(2,1)S(1)} %get-tuple-element.32), kind=kOutput, calls=%fused_computation.32 | convolution fusion | flops 269025280 | bytes 5275648 | tf_op jit(solution)/shard_map/xyq,rky->xrkq/dot_general | solution.py:40
  11.3 1.9 fusion.20
  13.2 9.1 %slice_negate_fusion = (bf16[4,4,32,64,64]{4,3,2,1,0:T(8,128)(2,1)S(1)}, bf16[4,4,32,64,64]{4,3,2,1,0:T(8,128)(2,1)S(1)}) fusion(bf16[4,4,32,64,128]{4,3,2,1,0:T(8,128)(2,1)} %param.6), kind=kLoop, calls=%fused_computation.23 | loop fusion | flops 2097152 | bytes 16777216 | tf_op jit(solution)/shard_map/neg | solution.py:48
  22.3 14.4 %maximum_maximum_fusion = bf16[4,4,32,128,128]{4,3,2,1,0:T(8,128)(2,1)} fusion(bf16[4,4,32,64,64]{4,3,2,1,0:T(8,128)(2,1)S(1)} %get-tuple-element.25, bf16[4,4,32,64,64]{4,3,2,1,0:T(8,128)(2,1)S(1)} %get-tuple-element.24, bf16[4,4,32,64,128]{4,3,2,1,0:T(8,128)(2,1)} %param.6), kind=kLoop, calls=%fused_computation.2 | loop fusion | flops 50331648 | bytes 33554432 | tf_op jit(solution)/shard_map/concatenate | solution.py:49
  36.7 15.4 %reduce-scatter.3.cloned.1.call-done = bf16[4,2,32,256]{3,2,1,0:T(8,128)(2,1)} async-done(((bf16[32,2,32,256]{3,2,1,0:T(8,128)(2,1)}), bf16[4,2,32,256]{3,2,1,0:T(8,128)(2,1)}) %reduce-scatter.3.cloned.1.call-update) | async-done | bytes 131088 | tf_op jit(solution)/shard_map/reduce_scatter | solution.py:95
  52.1 1.1 reshape.352
  53.6 8.0 %fusion.55 = f32[4,128,1,128]{3,2,1,0:T(1,128)S(1)} fusion(bf16[4,128,128,1]{2,3,1,0:T(2,128)(2,1)S(1)} %reshape.391, bf16[4,128,128,128]{3,2,1,0:T(8,128)(2,1)} %bitcast.167), kind=kOutput, calls=%fused_computation.97 | convolution fusion | flops 16777216 | bytes 17170432 | tf_op jit(solution)/shard_map/zmpi,zmio->zmpo/dot_general | solution.py:40
  62.0 0.9 reshape.356
  63.1 12.6 %copy.49 = bf16[32,256,1,4,64]{4,3,1,0,2:T(4,128)(2,1)} copy(bf16[32,256,1,4,64]{1,4,3,2,0:T(8,128)(2,1)} %param.4) | data formatting | bytes 8388608 | tf_op args[0]
  75.8 11.9 %fusion.56 = f32[32768,64]{1,0:T(8,128)} fusion(bf16[32768,64]{1,0:T(8,128)(2,1)} %bitcast.169, bf16[64,64]{1,0:T(8,128)(2,1)S(1)} %copy-done), kind=kOutput, calls=%fused_computation.98 | convolution fusion | flops 268435456 | bytes 12591104 | tf_op jit(solution)/shard_map/dot_general | solution.py:114
  87.6 14.3 %reshape.358 = f32[32,256,256]{2,1,0:T(8,128)} reshape(f32[32768,64]{1,0:T(8,128)} %fusion.56) | data formatting | bytes 16777216 | tf_op jit(solution)/shard_map/reshape | solution.py:117
  102.0 8.9 %copy.51 = f32[32,256,256]{1,2,0:T(8,128)} copy(f32[32,256,256]{2,1,0:T(8,128)} %reshape.358) | data formatting | bytes 16777216 | tf_op jit(solution)/shard_map/reshape | solution.py:117
  111.1 1.7 fusion.22
  112.8 12.0 %fusion.2 = (bf16[32,256,256]{1,2,0:T(8,128)(2,1)S(1)}, bf16[32,256,256]{1,2,0:T(8,128)(2,1)}) fusion(bf16[32,256,1,4,64]{1,4,3,2,0:T(8,128)(2,1)} %param.5, f32[32,256,256]{1,2,0:T(8,128)} %copy.51, f32[32]{0:T(128)S(1)} %compare_select_fusion, bf16[1,32,256]{2,1,0:T(8,128)(2,1)S(1)} %get-tuple-element.31, bf16[1,32,256]{2,1,0:T(8,128)(2,1)S(1)} %get-tuple-element.32, ...), kind=kOutput, calls=%fused_computation.11 | convolution fusion | flops 318832640 | bytes 22052992 | tf_op jit(solution)/shard_map/yrk,xrkq->xyq/dot_general | solution.py:40
  124.8 2.0 copy-done.2
  126.8 1.4 fusion.17
  128.2 6.4 %copy.58 = bf16[32,256,256]{2,1,0:T(8,128)(2,1)} copy(bf16[32,256,256]{1,2,0:T(8,128)(2,1)} %copy-done.2) | data formatting | bytes 8388608 | tf_op jit(solution)/shard_map/convert_element_type | solution.py:123
  134.6 1.9 fusion.21
  136.6 11.2 %reshape.364 = bf16[32768,64]{1,0:T(8,128)(2,1)} reshape(bf16[32,256,256]{2,1,0:T(8,128)(2,1)} %copy.58) | data formatting | bytes 8388608 | tf_op jit(solution)/shard_map/reshape | solution.py:139
  147.7 8.2 %convolution_bitcast_fusion = f32[64,64]{0,1:T(8,128)S(1)} fusion(bf16[32768,64]{1,0:T(8,128)(2,1)} %reshape.364, bf16[32768,64]{1,0:T(8,128)(2,1)} %bitcast.170), kind=kOutput, calls=%fused_computation.38 | convolution fusion | flops 268435456 | bytes 8404992 | tf_op jit(solution)/shard_map/dot_general | solution.py:124
  155.9 39.8 %psum.7 = f32[64,64]{0,1:T(8,128)S(1)} all-reduce(f32[64,64]{0,1:T(8,128)S(1)} %convolution_bitcast_fusion), channel_id=1, replica_groups=mesh['dp'=4,'mp'=8] {'dp','mp'}, use_global_device_ids=true, to_apply=%region_2.3 | all-reduce | flops 4096 | bytes 32768 | tf_op jit(solution)/shard_map/psum | solution.py:130
  196.4 11.9 %fusion.58 = f32[32768,64]{1,0:T(8,128)} fusion(bf16[32768,64]{1,0:T(8,128)(2,1)} %reshape.364, bf16[64,64]{1,0:T(8,128)(2,1)S(1)} %copy-done), kind=kOutput, calls=%fused_computation.100 | convolution fusion | flops 268435456 | bytes 12591104 | tf_op jit(solution)/shard_map/dot_general | solution.py:138
  208.2 14.4 %reshape.365 = f32[32,256,256]{2,1,0:T(8,128)} reshape(f32[32768,64]{1,0:T(8,128)} %fusion.58) | data formatting | bytes 16777216 | tf_op jit(solution)/shard_map/reshape | solution.py:141
  222.6 9.0 %copy.60 = f32[32,256,256]{1,2,0:T(8,128)} copy(f32[32,256,256]{2,1,0:T(8,128)} %reshape.365) | data formatting | bytes 16777216 | tf_op jit(solution)/shard_map/reshape | solution.py:141
  231.6 1.1 reshape.360
  233.3 12.2 %fusion.57 = f32[4,128,1,128]{3,2,1,0:T(1,128)S(1)} fusion(bf16[4,128,128,1]{2,3,1,0:T(2,128)(2,1)S(1)} %reshape.393, bf16[4,128,128,128]{3,2,1,0:T(8,128)(2,1)} %bitcast.168), kind=kOutput, calls=%fused_computation.99 | convolution fusion | flops 16777216 | bytes 17170432 | tf_op jit(solution)/shard_map/zmpo,zmio->zmpi/dot_general | solution.py:40
  245.9 0.9 reshape.363
  246.8 11.4 %broadcast_multiply_fusion = f32[4,128,128,128]{3,2,1,0:T(8,128)} fusion(f32[4,128,128]{2,1,0:T(8,128)S(1)} %convert.35, f32[4,128,128]{2,1,0:T(8,128)S(1)} %convert.34), kind=kLoop, calls=%fused_computation.4 | loop fusion | flops 8388608 | bytes 34078720 | tf_op jit(solution)/shard_map/zmpi,zmpo->zmio/dot_general | solution.py:40
  258.3 34.2 %slice_add_fusion = (f32[4,128,64,64]{3,2,1,0:T(8,128)}, f32[4,128,64,64]{3,2,1,0:T(8,128)}) fusion(f32[4,128,128,128]{3,2,1,0:T(8,128)} %broadcast_multiply_fusion), kind=kLoop, calls=%fused_computation.1 | loop fusion | flops 4194304 | bytes 50331648 | tf_op jit(solution)/shard_map/add | solution.py:77
  292.5 17.0 %pad_maximum_fusion = f32[4,128,64,128]{3,2,1,0:T(8,128)} fusion(f32[4,128,64,64]{3,2,1,0:T(8,128)} %get-tuple-element.21, f32[4,128,64,64]{3,2,1,0:T(8,128)} %get-tuple-element.20), kind=kLoop, calls=%fused_computation.3 | loop fusion | flops 4194304 | bytes 33554432 | tf_op jit(solution)/shard_map/concatenate | solution.py:77
  309.5 1.7 fusion.23
  311.2 7.5 %fusion.10 = bf16[32,256,256]{1,2,0:T(8,128)(2,1)} fusion(f32[32,256,256]{1,2,0:T(8,128)} %copy.60, bf16[32,2,32,256]{3,0,1,2:T(8,128)(2,1)S(1)} %fusion.23, bf16[1,32,256]{2,1,0:T(8,128)(2,1)S(1)} %get-tuple-element.31, bf16[1,32,256]{2,1,0:T(8,128)(2,1)S(1)} %get-tuple-element.32), kind=kOutput, calls=%fused_computation.20 | convolution fusion | flops 272646144 | bytes 13664256 | tf_op jit(solution)/shard_map/rky,xrkq->xyq/dot_general | solution.py:40
  (39 shorter events, 3.6 us)
Async XLA Ops:
  7.2 68.6 %copy-start = (bf16[64,64]{1,0:T(8,128)(2,1)S(1)}, bf16[64,64]{1,0:T(8,128)(2,1)}, u32[]{:S(2)}) copy-start(bf16[64,64]{1,0:T(8,128)(2,1)} %param.7) | copy-start | bytes 24580
  7.2 44.9 %reduce-scatter.3.cloned.1.call-start = ((), (), s32[]{:S(2)}) async-start(), calls=%async_computation.2 | async-start | bytes 1179648 | tf_op jit(solution)/shard_map/reduce_scatter | solution.py:95
  13.2 97.9 %all-gather.3.cloned.1.call-start = ((), (), s32[]{:S(2)}) async-start(), calls=%async_computation.3 | async-start | bytes 1179648 | tf_op jit(solution)/shard_map/all_gather | solution.py:104
  62.9 168.7 %reduce-scatter.5.cloned.1.call-start = ((), (), s32[]{:S(2)}) async-start(), calls=%async_computation.4 | async-start | bytes 1179648 | tf_op jit(solution)/shard_map/reduce_scatter | solution.py:95
  124.8 2.0 copy-start.2
  136.5 173.0 %all-gather.5.cloned.1.call-start = ((), (), s32[]{:S(2)}) async-start(), calls=%async_computation.5 | async-start | bytes 1179648 | tf_op jit(solution)/shard_map/all_gather | solution.py:104
  292.5 26.2 %copy-start.1 = (bf16[64,64]{1,0:T(8,128)(2,1)S(1)}, bf16[64,64]{1,0:T(8,128)(2,1)}, u32[]{:S(2)}) copy-start(bf16[64,64]{1,0:T(8,128)(2,1)} %param.7) | copy-start | bytes 24580
Sparse Core Ops, SparseCore 0:
  13.3 38.7 reduce-scatter.2
  63.0 23.4 all-gather.2
  136.6 36.3 reduce-scatter.4
  246.9 24.1 all-gather.4
where the time goes:
time: 328 us; the launch traced here: 325 us
  other arithmetic  86.7 us (26%)
  local copies, waits for them, and re-layouts  85.2 us (26%)
  matrix products  83.7 us (26%)
  blocking collectives  39.8 us (12%)
  waiting for transfers between devices  15.5 us (5%)
  between operations  14 us (4%)
    dot_general x10, matrix products, product(): return jnp.einsum(form, left, right, preferred_element_type=jnp.float32)  51.8 us
    psum x1, blocking collectives, body(): local_grad = lax.psum(local_term, ('dp', 'mp')) * grad_scale  39.8 us
    add x1, other arithmetic, combine(): joined = jnp.concatenate([top_left + low_right, top_right - low_left], -1)  34.2 us
    reshape x2, local copies, waits for them, and re-layouts, body(): local_back.reshape(rows_here, grid_y, columns)  23.4 us
    reshape x2, local copies, waits for them, and re-layouts, body(): local_part.reshape(rows_here, grid_y, columns)  23.3 us
    concatenate x1, other arithmetic, combine(): joined = jnp.concatenate([top_left + low_right, top_right - low_left], -1)  17 us
    reduce_scatter x2, waiting for transfers between devices, to_modes(): lax.psum_scatter(product('ojrx,xrkq->kojq', x_table_own, spectrum).astype...  15.4 us
    unnamed x8, local copies, waits for them, and re-layouts  15.3 us
  transfers between devices with their start and end apart: 4, of which 1 were waited for; matrix products, arithmetic and copies ran while one was open for 58% of the time, Pallas kernels for 0%

commit v1 on v0

--- a/solution.py
+++ b/solution.py
@@ -127,7 +127,7 @@
         preferred_element_type=jnp.float32,
     )
     grad_scale = 1.0 / math.sqrt(NX * NY * SNAP * lax.axis_size("dp") * zcount)
-    local_grad = lax.psum(local_term, ("dp", "mp")) * grad_scale
+    local_grad = lax.psum(lax.psum(local_term, "dp"), "mp") * grad_scale
     rows_grad = product("yrk,xyq->xrkq", y_back, preact_grad).astype(jnp.bfloat16)
     mixed_grad = to_modes(rows_grad)
     grad_items = to_items(mixed_grad, snaps, zcount)

time: 328 us -> 330 us (level)
    psum x1 -> x2, blocking collectives: 39.8 us -> 41.7 us  [body(): local_grad = lax.psum(lax.psum(local_term, 'dp'), 'mp') * grad_scale]
where the time goes in v1:
time: 330 us; the launch traced here: 327 us
  other arithmetic  86.8 us (26%)
  local copies, waits for them, and re-layouts  85.2 us (26%)
  matrix products  83.6 us (25%)
  blocking collectives  41.7 us (13%)
  waiting for transfers between devices  15.5 us (5%)
  between operations  14 us (4%)
    dot_general x10, matrix products, product(): return jnp.einsum(form, left, right, preferred_element_type=jnp.float32)  51.7 us
    psum x2, blocking collectives, body(): local_grad = lax.psum(lax.psum(local_term, 'dp'), 'mp') * grad_scale  41.7 us
    add x1, other arithmetic, combine(): joined = jnp.concatenate([top_left + low_right, top_right - low_left], -1)  34.3 us
    reshape x2, local copies, waits for them, and re-layouts, body(): local_back.reshape(rows_here, grid_y, columns)  23.4 us
    reshape x2, local copies, waits for them, and re-layouts, body(): local_part.reshape(rows_here, grid_y, columns)  23.3 us
    concatenate x1, other arithmetic, combine(): joined = jnp.concatenate([top_left + low_right, top_right - low_left], -1)  17 us
    reduce_scatter x2, waiting for transfers between devices, to_modes(): lax.psum_scatter(product('ojrx,xrkq->kojq', x_table_own, spectrum).astype...  15.4 us
    unnamed x8, local copies, waits for them, and re-layouts  15.3 us
  transfers between devices with their start and end apart: 4, of which 1 were waited for; matrix products, arithmetic and copies ran while one was open for 58% of the time, Pallas kernels for 0%

profile of v1, /device:TPU:0, one launch (start us, length us, event | category | flops | bytes accessed | tf_op | source)
XLA Modules:
  0.0 327.1 jit_solution(12823412788867126916)
XLA Ops:
  7.7 3.6 %fusion.16 = bf16[32,2,32,256,1]{3,2,0,1,4:T(8,128)(2,1)S(1)} fusion(bf16[32,256,256,1]{1,2,0,3:T(8,128)(2,1)} %bitcast.172, bf16[1,32,256]{2,1,0:T(8,128)(2,1)S(1)} %get-tuple-element.31, bf16[1,32,256]{2,1,0:T(8,128)(2,1)S(1)} %get-tuple-element.32), kind=kOutput, calls=%fused_computation.32 | convolution fusion | flops 269025280 | bytes 5275648 | tf_op jit(solution)/shard_map/xyq,rky->xrkq/dot_general | solution.py:40
  11.3 1.9 fusion.20
  13.2 9.1 %slice_negate_fusion = (bf16[4,4,32,64,64]{4,3,2,1,0:T(8,128)(2,1)S(1)}, bf16[4,4,32,64,64]{4,3,2,1,0:T(8,128)(2,1)S(1)}) fusion(bf16[4,4,32,64,128]{4,3,2,1,0:T(8,128)(2,1)} %param.6), kind=kLoop, calls=%fused_computation.23 | loop fusion | flops 2097152 | bytes 16777216 | tf_op jit(solution)/shard_map/neg | solution.py:48
  22.3 14.4 %maximum_maximum_fusion = bf16[4,4,32,128,128]{4,3,2,1,0:T(8,128)(2,1)} fusion(bf16[4,4,32,64,64]{4,3,2,1,0:T(8,128)(2,1)S(1)} %get-tuple-element.25, bf16[4,4,32,64,64]{4,3,2,1,0:T(8,128)(2,1)S(1)} %get-tuple-element.24, bf16[4,4,32,64,128]{4,3,2,1,0:T(8,128)(2,1)} %param.6), kind=kLoop, calls=%fused_computation.2 | loop fusion | flops 50331648 | bytes 33554432 | tf_op jit(solution)/shard_map/concatenate | solution.py:49
  36.7 15.4 %reduce-scatter.3.cloned.1.call-done = bf16[4,2,32,256]{3,2,1,0:T(8,128)(2,1)} async-done(((bf16[32,2,32,256]{3,2,1,0:T(8,128)(2,1)}), bf16[4,2,32,256]{3,2,1,0:T(8,128)(2,1)}) %reduce-scatter.3.cloned.1.call-update) | async-done | bytes 131088 | tf_op jit(solution)/shard_map/reduce_scatter | solution.py:95
  52.1 1.1 reshape.352
  53.6 8.0 %fusion.55 = f32[4,128,1,128]{3,2,1,0:T(1,128)S(1)} fusion(bf16[4,128,128,1]{2,3,1,0:T(2,128)(2,1)S(1)} %reshape.391, bf16[4,128,128,128]{3,2,1,0:T(8,128)(2,1)} %bitcast.167), kind=kOutput, calls=%fused_computation.97 | convolution fusion | flops 16777216 | bytes 17170432 | tf_op jit(solution)/shard_map/zmpi,zmio->zmpo/dot_general | solution.py:40
  62.0 0.9 reshape.356
  63.1 12.6 %copy.49 = bf16[32,256,1,4,64]{4,3,1,0,2:T(4,128)(2,1)} copy(bf16[32,256,1,4,64]{1,4,3,2,0:T(8,128)(2,1)} %param.4) | data formatting | bytes 8388608 | tf_op args[0]
  75.7 11.9 %fusion.56 = f32[32768,64]{1,0:T(8,128)} fusion(bf16[32768,64]{1,0:T(8,128)(2,1)} %bitcast.169, bf16[64,64]{1,0:T(8,128)(2,1)S(1)} %copy-done), kind=kOutput, calls=%fused_computation.98 | convolution fusion | flops 268435456 | bytes 12591104 | tf_op jit(solution)/shard_map/dot_general | solution.py:114
  87.6 14.3 %reshape.358 = f32[32,256,256]{2,1,0:T(8,128)} reshape(f32[32768,64]{1,0:T(8,128)} %fusion.56) | data formatting | bytes 16777216 | tf_op jit(solution)/shard_map/reshape | solution.py:117
  101.9 8.9 %copy.51 = f32[32,256,256]{1,2,0:T(8,128)} copy(f32[32,256,256]{2,1,0:T(8,128)} %reshape.358) | data formatting | bytes 16777216 | tf_op jit(solution)/shard_map/reshape | solution.py:117
  111.1 1.7 fusion.22
  112.8 11.9 %fusion.2 = (bf16[32,256,256]{1,2,0:T(8,128)(2,1)S(1)}, bf16[32,256,256]{1,2,0:T(8,128)(2,1)}) fusion(bf16[32,256,1,4,64]{1,4,3,2,0:T(8,128)(2,1)} %param.5, f32[32,256,256]{1,2,0:T(8,128)} %copy.51, f32[32]{0:T(128)S(1)} %compare_select_fusion, bf16[1,32,256]{2,1,0:T(8,128)(2,1)S(1)} %get-tuple-element.31, bf16[1,32,256]{2,1,0:T(8,128)(2,1)S(1)} %get-tuple-element.32, ...), kind=kOutput, calls=%fused_computation.11 | convolution fusion | flops 318832640 | bytes 22052992 | tf_op jit(solution)/shard_map/yrk,xrkq->xyq/dot_general | solution.py:40
  124.8 2.0 copy-done.2
  126.8 1.4 fusion.17
  128.2 6.4 %copy.58 = bf16[32,256,256]{2,1,0:T(8,128)(2,1)} copy(bf16[32,256,256]{1,2,0:T(8,128)(2,1)} %copy-done.2) | data formatting | bytes 8388608 | tf_op jit(solution)/shard_map/convert_element_type | solution.py:123
  134.6 1.9 fusion.21
  136.5 11.1 %reshape.364 = bf16[32768,64]{1,0:T(8,128)(2,1)} reshape(bf16[32,256,256]{2,1,0:T(8,128)(2,1)} %copy.58) | data formatting | bytes 8388608 | tf_op jit(solution)/shard_map/reshape | solution.py:139
  147.7 8.2 %convolution_bitcast_fusion = f32[64,64]{0,1:T(8,128)S(1)} fusion(bf16[32768,64]{1,0:T(8,128)(2,1)} %reshape.364, bf16[32768,64]{1,0:T(8,128)(2,1)} %bitcast.170), kind=kOutput, calls=%fused_computation.38 | convolution fusion | flops 268435456 | bytes 8404992 | tf_op jit(solution)/shard_map/dot_general | solution.py:124
  155.9 19.1 %psum.14 = f32[64,64]{0,1:T(8,128)S(1)} all-reduce(f32[64,64]{0,1:T(8,128)S(1)} %convolution_bitcast_fusion), channel_id=1, replica_groups=mesh['dp'=4,'mp'=8] {'dp'}, use_global_device_ids=true, to_apply=%region_2.3 | all-reduce | flops 4096 | bytes 32768 | tf_op jit(solution)/shard_map/psum | solution.py:130
  175.0 22.6 %psum.15 = f32[64,64]{0,1:T(8,128)S(1)} all-reduce(f32[64,64]{0,1:T(8,128)S(1)} %psum.14), channel_id=1, replica_groups=mesh['dp'=4,'mp'=8] {'mp'}, use_global_device_ids=true, to_apply=%region_3.4 | all-reduce | flops 4096 | bytes 32768 | tf_op jit(solution)/shard_map/psum | solution.py:130
  198.3 11.9 %fusion.58 = f32[32768,64]{1,0:T(8,128)} fusion(bf16[32768,64]{1,0:T(8,128)(2,1)} %reshape.364, bf16[64,64]{1,0:T(8,128)(2,1)S(1)} %copy-done), kind=kOutput, calls=%fused_computation.100 | convolution fusion | flops 268435456 | bytes 12591104 | tf_op jit(solution)/shard_map/dot_general | solution.py:138
  210.1 14.4 %reshape.365 = f32[32,256,256]{2,1,0:T(8,128)} reshape(f32[32768,64]{1,0:T(8,128)} %fusion.58) | data formatting | bytes 16777216 | tf_op jit(solution)/shard_map/reshape | solution.py:141
  224.5 9.0 %copy.60 = f32[32,256,256]{1,2,0:T(8,128)} copy(f32[32,256,256]{2,1,0:T(8,128)} %reshape.365) | data formatting | bytes 16777216 | tf_op jit(solution)/shard_map/reshape | solution.py:141
  233.5 1.1 reshape.360
  235.2 12.2 %fusion.57 = f32[4,128,1,128]{3,2,1,0:T(1,128)S(1)} fusion(bf16[4,128,128,1]{2,3,1,0:T(2,128)(2,1)S(1)} %reshape.393, bf16[4,128,128,128]{3,2,1,0:T(8,128)(2,1)} %bitcast.168), kind=kOutput, calls=%fused_computation.99 | convolution fusion | flops 16777216 | bytes 17170432 | tf_op jit(solution)/shard_map/zmpo,zmio->zmpi/dot_general | solution.py:40
  248.8 11.4 %broadcast_multiply_fusion = f32[4,128,128,128]{3,2,1,0:T(8,128)} fusion(f32[4,128,128]{2,1,0:T(8,128)S(1)} %convert.35, f32[4,128,128]{2,1,0:T(8,128)S(1)} %convert.34), kind=kLoop, calls=%fused_computation.4 | loop fusion | flops 8388608 | bytes 34078720 | tf_op jit(solution)/shard_map/zmpi,zmpo->zmio/dot_general | solution.py:40
  260.2 34.3 %slice_add_fusion = (f32[4,128,64,64]{3,2,1,0:T(8,128)}, f32[4,128,64,64]{3,2,1,0:T(8,128)}) fusion(f32[4,128,128,128]{3,2,1,0:T(8,128)} %broadcast_multiply_fusion), kind=kLoop, calls=%fused_computation.1 | loop fusion | flops 4194304 | bytes 50331648 | tf_op jit(solution)/shard_map/add | solution.py:77
  294.5 17.0 %pad_maximum_fusion = f32[4,128,64,128]{3,2,1,0:T(8,128)} fusion(f32[4,128,64,64]{3,2,1,0:T(8,128)} %get-tuple-element.21, f32[4,128,64,64]{3,2,1,0:T(8,128)} %get-tuple-element.20), kind=kLoop, calls=%fused_computation.3 | loop fusion | flops 4194304 | bytes 33554432 | tf_op jit(solution)/shard_map/concatenate | solution.py:77
  311.5 1.7 fusion.23
  313.2 7.4 %fusion.10 = bf16[32,256,256]{1,2,0:T(8,128)(2,1)} fusion(f32[32,256,256]{1,2,0:T(8,128)} %copy.60, bf16[32,2,32,256]{3,0,1,2:T(8,128)(2,1)S(1)} %fusion.23, bf16[1,32,256]{2,1,0:T(8,128)(2,1)S(1)} %get-tuple-element.31, bf16[1,32,256]{2,1,0:T(8,128)(2,1)S(1)} %get-tuple-element.32), kind=kOutput, calls=%fused_computation.20 | convolution fusion | flops 272646144 | bytes 13664256 | tf_op jit(solution)/shard_map/rky,xrkq->xyq/dot_general | solution.py:40
  (40 shorter events, 4.4 us)
Async XLA Ops:
  7.2 68.6 %copy-start = (bf16[64,64]{1,0:T(8,128)(2,1)S(1)}, bf16[64,64]{1,0:T(8,128)(2,1)}, u32[]{:S(2)}) copy-start(bf16[64,64]{1,0:T(8,128)(2,1)} %param.7) | copy-start | bytes 24580
  7.2 44.9 %reduce-scatter.3.cloned.1.call-start = ((), (), s32[]{:S(2)}) async-start(), calls=%async_computation.2 | async-start | bytes 1179648 | tf_op jit(solution)/shard_map/reduce_scatter | solution.py:95
  13.2 97.9 %all-gather.3.cloned.1.call-start = ((), (), s32[]{:S(2)}) async-start(), calls=%async_computation.3 | async-start | bytes 1179648 | tf_op jit(solution)/shard_map/all_gather | solution.py:104
  62.9 170.6 %reduce-scatter.5.cloned.1.call-start = ((), (), s32[]{:S(2)}) async-start(), calls=%async_computation.4 | async-start | bytes 1179648 | tf_op jit(solution)/shard_map/reduce_scatter | solution.py:95
  124.7 2.0 copy-start.2
  136.5 175.0 %all-gather.5.cloned.1.call-start = ((), (), s32[]{:S(2)}) async-start(), calls=%async_computation.5 | async-start | bytes 1179648 | tf_op jit(solution)/shard_map/all_gather | solution.py:104
  294.5 26.1 %copy-start.1 = (bf16[64,64]{1,0:T(8,128)(2,1)S(1)}, bf16[64,64]{1,0:T(8,128)(2,1)}, u32[]{:S(2)}) copy-start(bf16[64,64]{1,0:T(8,128)(2,1)} %param.7) | copy-start | bytes 24580
Sparse Core Ops, SparseCore 0:
  13.3 38.7 reduce-scatter.2
  63.0 23.4 all-gather.2
  136.6 36.0 reduce-scatter.4
  248.8 20.6 all-gather.4
